TPU v7x, 512 devices: a whole 4x8x8 slice. The times are simulated.
512 devices in a mesh: dp: 4 (over x_lo, core), blk: 128 (over y, z, x_hi).
Axes of the slice: x: 4 (x_hi: 2, x_lo: 2; x = x_hi * 2 + x_lo), y: 8, z: 8, core: 2. Of those that a mesh axis runs over, the one named last changes fastest.
Arguments:
- queries: bfloat16 [4, 24576, 512], P('dp', 'blk'), may hold values from -6 to 6, as said below
- key_in: bfloat16 [4, 24576, 512], P('dp', 'blk'), may hold values from -6 to 6, as said below
- value_in: bfloat16 [4, 24576, 512], P('dp', 'blk'), may hold values from -6 to 6
- out_weight: bfloat16 [512, 1024], replicated, may hold values from -2 to 2
- conv_kernel: float32 [31, 1024], replicated, may hold values from -1 to 1
- cotangent: bfloat16 [4, 24576, 1024], P('dp', 'blk'), may hold values from -6 to 6
Outputs:
- out_frames: bfloat16 [4, 24576, 1024], P('dp', 'blk')
- query_grad: bfloat16 [4, 24576, 512], P('dp', 'blk')
- key_grad: bfloat16 [4, 24576, 512], P('dp', 'blk')
- value_grad: bfloat16 [4, 24576, 512], P('dp', 'blk')
- weight_grad: float32 [512, 1024], replicated
- kernel_grad: float32 [31, 1024], replicated
Inputs may be any that keep to these rules, and one draw needn't show every extreme that they name: `queries`: independent entries. `key_in`: independent entries.
All inputs are finite; a program needn't handle non-finite values.
Results may differ from a plain program's by a relative error of at most 0.024.
Values may be sent and summed in bfloat16 or wider, within the bound.
A program may use at most 64 MiB of HBM per device.

v0:
```python
import math
import jax
import jax.numpy as jnp
from jax import lax
from jax.sharding import PartitionSpec as P

ATT_HEADS = 8
HEAD_DIM = 64
CTX_MAX = 3
ATT = 512
NEGATIVE = -1e30


def from_behind(block, axis, distance):
    devices = range(lax.axis_size(axis))
    route = [(i - distance, i) for i in devices if i - distance in devices]
    return lax.ppermute(block, axis, route)


def split_heads(matrix):
    return matrix.reshape(matrix.shape[0], ATT_HEADS, HEAD_DIM)


def tile_scores(query_heads, tile, query_pos, key_pos, usable, left_span, score_scale):
    key_heads = split_heads(tile[:, :ATT])
    scores = (
        jnp.einsum("qhd,khd->hqk", query_heads, key_heads, preferred_element_type=jnp.float32)
        * score_scale
    )
    distance = query_pos[:, None] - key_pos[None, :]
    visible = ((distance >= 0) & (distance < left_span) & usable)[None]
    return (jnp.where(visible, scores, NEGATIVE), visible)


def attend_tile(
    softmax_state, query_heads, tile, query_pos, key_pos, usable, left_span, score_scale
):
    running_max, running_sum, weighted = softmax_state
    scores, visible = tile_scores(
        query_heads, tile, query_pos, key_pos, usable, left_span, score_scale
    )
    new_max = jnp.maximum(running_max, jnp.max(scores, axis=-1))
    weights = jnp.where(visible, jnp.exp(scores - new_max[..., None]), 0.0)
    fading = jnp.exp(running_max - new_max)
    running_sum = running_sum * fading + jnp.sum(weights, axis=-1)
    value_heads = split_heads(tile[:, ATT:])
    update = jnp.einsum(
        "hqk,khd->qhd",
        weights.astype(jnp.bfloat16),
        value_heads,
        preferred_element_type=jnp.float32,
    )
    weighted = weighted * jnp.transpose(fading)[:, :, None] + update
    return (new_max, running_sum, weighted)


def tile_grads(
    query_heads,
    dout_heads,
    log_sums,
    deltas,
    tile,
    query_pos,
    key_pos,
    usable,
    left_span,
    score_scale,
):
    scores, visible = tile_scores(
        query_heads, tile, query_pos, key_pos, usable, left_span, score_scale
    )
    key_heads = split_heads(tile[:, :ATT])
    value_heads = split_heads(tile[:, ATT:])
    probs = jnp.where(visible, jnp.exp(scores - log_sums[..., None]), 0.0)
    dvalue_heads = jnp.einsum(
        "hqk,qhd->khd", probs.astype(jnp.bfloat16), dout_heads, preferred_element_type=jnp.float32
    )
    dprobs = jnp.einsum("qhd,khd->hqk", dout_heads, value_heads, preferred_element_type=jnp.float32)
    dscores = (probs * (dprobs - deltas[..., None])).astype(jnp.bfloat16)
    dquery = (
        jnp.einsum("hqk,khd->qhd", dscores, key_heads, preferred_element_type=jnp.float32)
        * score_scale
    )
    dkey_heads = (
        jnp.einsum("hqk,qhd->khd", dscores, query_heads, preferred_element_type=jnp.float32)
        * score_scale
    )
    row_count = tile.shape[0]
    return (
        dquery,
        jnp.concatenate(
            [dkey_heads.reshape(row_count, ATT), dvalue_heads.reshape(row_count, ATT)], axis=1
        ),
    )


def depthwise(extended, conv_kernel, row_count, ahead):
    tap_count = conv_kernel.shape[0]

    def add_tap(tap_index, running):
        first_row = tap_index if ahead else tap_count - 1 - tap_index
        return running + conv_kernel[tap_index] * lax.dynamic_slice_in_dim(
            extended, first_row, row_count, 0
        )

    empty = jnp.zeros((row_count, extended.shape[1]), jnp.float32)
    return lax.fori_loop(0, tap_count, add_tap, empty)


def sum_weights(weight_part, kernel_part):
    return lax.psum((weight_part, kernel_part), ("dp", "blk"))


def per_device(queries, key_in, value_in, out_weight, conv_kernel, cotangent):
    cycle_count = lax.axis_size("blk")
    device = lax.axis_index("blk")
    row_count = queries.shape[1]
    context = min(CTX_MAX, cycle_count // 4)
    left_span = context * row_count
    score_scale = 1.0 / math.sqrt(HEAD_DIM)
    edge_rows = conv_kernel.shape[0] - 1
    row_ids = jnp.arange(row_count, dtype=jnp.int32)
    query_heads = split_heads(queries[0])
    own_tile = jnp.concatenate([key_in[0], value_in[0]], axis=1)
    own_pos = device * row_count + row_ids
    always = jnp.array(True)

    def source(offset):
        anchor = device - offset
        return (anchor * row_count + row_ids, anchor >= 0)

    start_state = (
        jnp.full((ATT_HEADS, row_count), NEGATIVE, jnp.float32),
        jnp.zeros((ATT_HEADS, row_count), jnp.float32),
        jnp.zeros((row_count, ATT_HEADS, HEAD_DIM), jnp.float32),
    )
    first_state = attend_tile(
        start_state, query_heads, own_tile, own_pos, own_pos, always, left_span, score_scale
    )

    def forward_step(carry, offset):
        moving, softmax_state = carry
        arrived = from_behind(moving, "blk", 1)
        tile_pos, tile_usable = source(offset)
        softmax_state = attend_tile(
            softmax_state,
            query_heads,
            arrived,
            own_pos,
            tile_pos,
            tile_usable,
            left_span,
            score_scale,
        )
        return ((arrived, softmax_state), arrived)

    offsets = jnp.arange(1, context + 1, dtype=jnp.int32)
    (unused_tile, final_state), kept_tiles = lax.scan(
        forward_step, (own_tile, first_state), offsets
    )
    running_max, running_sum, weighted = final_state
    attended = (weighted / jnp.transpose(running_sum)[:, :, None]).astype(jnp.bfloat16)
    log_sums = running_max + jnp.log(running_sum)
    flat = attended.reshape(row_count, ATT)
    hidden = jnp.dot(flat, out_weight, preferred_element_type=jnp.float32).astype(jnp.bfloat16)
    before = from_behind(hidden[-edge_rows:], "blk", 1)
    extended = jnp.concatenate([before, hidden], axis=0).astype(jnp.float32)
    mixed = depthwise(extended, conv_kernel, row_count, False)
    sigma = jax.nn.sigmoid(mixed)
    out_frames = (mixed * sigma).astype(jnp.bfloat16)[None]
    upstream = cotangent[0].astype(jnp.float32)
    dmixed = upstream * sigma * (1.0 + mixed * (1.0 - sigma))
    after = from_behind(dmixed[:edge_rows].astype(jnp.bfloat16), "blk", -1).astype(jnp.float32)
    dextended = jnp.concatenate([dmixed, after], axis=0)
    dhidden = depthwise(dextended, conv_kernel, row_count, True).astype(jnp.bfloat16)

    def kernel_tap(tap_index):
        window = lax.dynamic_slice_in_dim(extended, edge_rows - tap_index, row_count, 0)
        return jnp.sum(dmixed * window, axis=0)

    kernel_part = lax.map(kernel_tap, jnp.arange(edge_rows + 1, dtype=jnp.int32))
    weight_part = jnp.einsum("ra,rd->ad", flat, dhidden, preferred_element_type=jnp.float32)
    dattended = jnp.einsum(
        "rd,ad->ra", dhidden, out_weight, preferred_element_type=jnp.float32
    ).astype(jnp.bfloat16)
    dout_heads = split_heads(dattended)
    deltas = jnp.einsum("rhe,rhe->hr", dout_heads, attended, preferred_element_type=jnp.float32)
    dquery_own, dkv_own = tile_grads(
        query_heads,
        dout_heads,
        log_sums,
        deltas,
        own_tile,
        own_pos,
        own_pos,
        always,
        left_span,
        score_scale,
    )
    zero_buffer = jnp.zeros((row_count, 2 * ATT), jnp.float32)

    def backward_step(carry, inputs):
        buffer, dquery_sum = carry
        tile, offset = inputs
        tile_pos, tile_usable = source(offset)
        dquery_part, dkv_part = tile_grads(
            query_heads,
            dout_heads,
            log_sums,
            deltas,
            tile,
            own_pos,
            tile_pos,
            tile_usable,
            left_span,
            score_scale,
        )
        arrived = from_behind((buffer + dkv_part).astype(jnp.bfloat16), "blk", -1).astype(
            jnp.float32
        )
        return ((arrived, dquery_sum + dquery_part), None)

    (buffer, dquery_sum), unused = lax.scan(
        backward_step, (zero_buffer, dquery_own), (kept_tiles, offsets), reverse=True
    )
    dkv_total = dkv_own + buffer
    weight_total, kernel_total = sum_weights(weight_part, kernel_part)
    query_grad = dquery_sum.reshape(row_count, ATT).astype(jnp.bfloat16)[None]
    key_grad = dkv_total[:, :ATT].astype(jnp.bfloat16)[None]
    value_grad = dkv_total[:, ATT:].astype(jnp.bfloat16)[None]
    return (out_frames, query_grad, key_grad, value_grad, weight_total, kernel_total)


def solution(mesh):
    return jax.shard_map(
        per_device,
        mesh=mesh,
        in_specs=(
            P("dp", "blk", None),
            P("dp", "blk", None),
            P("dp", "blk", None),
            P(),
            P(),
            P("dp", "blk", None),
        ),
        out_specs=(
            P("dp", "blk", None),
            P("dp", "blk", None),
            P("dp", "blk", None),
            P("dp", "blk", None),
            P(),
            P(),
        ),
        check_vma=False,
    )
```

profile of v0, /device:TPU:24, one launch (start us, length us, event | category | flops | bytes accessed | tf_op | source)
XLA Modules:
  0.0 622.3 jit_solution(3382806898935224929)
XLA Ops:
  12.4 69.9 %while.79 = (s32[]{:T(128)}, bf16[192,1024]{0,1:T(8,128)(2,1)S(1)}, f32[8,192]{1,0:T(8,128)S(1)}, f32[8,192]{1,0:T(8,128)S(1)}, f32[192,8,64]{0,2,1:T(8,128)S(1)...) while((s32[]{:T(128)}, bf16[192,1024]{0,1:T(8,128)(2,1)S(1)}, ...), condition=%wide.region_5.6_spmd.clone, body=%wide.region_2.5_spmd.clone.sunk | while | flops 78537600 | bytes 9227495 | solution.py:158
  12.4 4.9 collective-permute-start
  18.7 18.9 %collective-permute-done = bf16[192,1024]{0,1:T(8,128)(2,1)S(1)} collective-permute-done((bf16[192,1024]{0,1:T(8,128)(2,1)S(1)}, bf16[192,1024]{0,1:T(8,128)(2,1)S(1)}, u32[]{:S(2)}, u32[]{:S(2)}) %collective-permute-start) | collective-permute-done | bytes 393248 | tf_op jit(solution)/shard_map/while/body/eval_jaxpr/ppermute | solution.py:17
  39.8 1.9 collective-permute-start
  43.1 16.2 %collective-permute-done = bf16[192,1024]{0,1:T(8,128)(2,1)S(1)} collective-permute-done((bf16[192,1024]{0,1:T(8,128)(2,1)S(1)}, bf16[192,1024]{0,1:T(8,128)(2,1)S(1)}, u32[]{:S(2)}, u32[]{:S(2)}) %collective-permute-start) | collective-permute-done | bytes 393248 | tf_op jit(solution)/shard_map/while/body/eval_jaxpr/ppermute | solution.py:17
  61.5 1.9 collective-permute-start
  64.8 15.3 %collective-permute-done = bf16[192,1024]{0,1:T(8,128)(2,1)S(1)} collective-permute-done((bf16[192,1024]{0,1:T(8,128)(2,1)S(1)}, bf16[192,1024]{0,1:T(8,128)(2,1)S(1)}, u32[]{:S(2)}, u32[]{:S(2)}) %collective-permute-start) | collective-permute-done | bytes 393248 | tf_op jit(solution)/shard_map/while/body/eval_jaxpr/ppermute | solution.py:17
  82.8 1.9 collective-permute-start.2
  84.9 8.7 %collective-permute-done.2 = bf16[30,1024]{1,0:T(8,128)(2,1)S(1)} collective-permute-done((bf16[30,1024]{1,0:T(8,128)(2,1)S(1)}, bf16[30,1024]{1,0:T(8,128)(2,1)S(1)}, u32[]{:S(2)}, u32[]{:S(2)}) %collective-permute-start.2) | collective-permute-done | bytes 61472 | tf_op jit(solution)/shard_map/ppermute | solution.py:17
  94.6 36.2 %while.80 = (s32[]{:T(128)}, f32[192,1024]{1,0:T(8,128)S(1)}, f32[31,1024]{1,0:T(8,128)}, f32[222,1024]{1,0:T(8,128)S(1)}, s32[]{:T(128)}, /*index=5*/s32[]{:T(128)}, s32[]{:T(128)}, s32[]{:T(128)}) while((s32[]{:T(128)}, f32[192,1024]{1,0:T(8,128)S(1)}, f32[31,1024]{1,0:T(8,128)}, f32[222,1024]{1,0:T(8,128)S(1)}, s32[]{:T(128)}, ...), condition=%wide.region_7.8_spmd.clone, body=%wide.region_6.7_spmd.clone.sunk | while | flops 589831 | bytes 2371741 | solution.py:107
  131.7 2.3 fusion.39
  134.1 1.9 collective-permute-start.3
  136.0 106.3 %while.78 = (s32[]{:T(128)}, f32[31,1024]{1,0:T(8,128)}, s32[31]{0:T(128)S(1)}, f32[222,1024]{1,0:T(8,128)S(1)}, f32[192,1024]{1,0:T(8,128)S(1)}, /*index=5*/s32[]{:T(128)}, s32[1]{0:T(128)}, s32[]{:T(128)}, s32[1]{0:T(128)}) while((s32[]{:T(128)}, f32[31,1024]{1,0:T(8,128)}, s32[31]{0:T(128)S(1)}, f32[222,1024]{1,0:T(8,128)S(1)}, ...), condition=%wide.region_15.16_spmd, body=%wide.region_13.15_spmd.sunk | while | flops 392198 | bytes 1585319 | solution.py:181
  138.1 1.4 dynamic_update_slice.15
  144.9 1.4 dynamic_update_slice.15
  151.8 1.4 dynamic_update_slice.15
  155.2 1.4 dynamic_update_slice.15
  162.1 1.4 dynamic_update_slice.15
  243.8 71.2 %while.81 = (s32[]{:T(128)}, f32[192,1024]{1,0:T(8,128)S(1)}, f32[31,1024]{1,0:T(8,128)}, f32[222,1024]{1,0:T(8,128)}, s32[]{:T(128)}, /*index=5*/s32[]{:T(128)}) while((s32[]{:T(128)}, f32[192,1024]{1,0:T(8,128)S(1)}, f32[31,1024]{1,0:T(8,128)}, f32[222,1024]{1,0:T(8,128)}, s32[]{:T(128)}, /*index=5*/s32[]{:T(128)}) %tuple.190), condition=%wide.region_9.10_spmd.clone, body=%wide.region_8.9_spmd.clone.sunk | while | flops 589827 | bytes 2371679 | solution.py:107
  244.6 1.5 select_add_fusion.5
  246.9 1.5 select_add_fusion.5
  249.2 1.5 select_add_fusion.5
  251.5 1.5 select_add_fusion.5
  253.8 1.5 select_add_fusion.5
  256.1 1.5 select_add_fusion.5
  258.4 1.5 select_add_fusion.5
  260.7 1.5 select_add_fusion.5
  263.0 1.5 select_add_fusion.5
  265.2 1.5 select_add_fusion.5
  267.5 1.5 select_add_fusion.5
  269.8 1.5 select_add_fusion.5
  272.1 1.5 select_add_fusion.5
  274.4 1.5 select_add_fusion.5
  276.7 1.5 select_add_fusion.5
  279.0 1.5 select_add_fusion.5
  281.3 1.5 select_add_fusion.5
  283.6 1.5 select_add_fusion.5
  285.9 1.5 select_add_fusion.5
  288.2 1.5 select_add_fusion.5
  290.5 1.5 select_add_fusion.5
  292.8 1.5 select_add_fusion.5
  295.1 1.5 select_add_fusion.5
  297.4 1.5 select_add_fusion.5
  299.7 1.5 select_add_fusion.5
  302.0 1.5 select_add_fusion.5
  304.3 1.5 select_add_fusion.5
  306.6 1.5 select_add_fusion.5
  308.9 1.5 select_add_fusion.5
  311.2 1.5 select_add_fusion.5
  313.5 1.5 select_add_fusion.5
  315.9 2.4 convolution_convert_fusion.1
  324.2 1.8 fusion.48
  328.3 63.4 %while.82 = (s32[]{:T(128)}, f32[192,1024]{0,1:T(8,128)S(1)}, f32[192,8,64]{0,2,1:T(8,128)}, s32[3]{0:T(128)S(1)}, s32[]{:T(128)}, /*index=5*/bf16[3,192,1024]{1...) while((s32[]{:T(128)}, f32[192,1024]{0,1:T(8,128)S(1)}, ...), condition=%wide.region_11.12_spmd.clone, body=%wide.region_10.11_spmd.clone.sunk | while | flops 192565632 | bytes 15424801 | solution.py:223
  333.5 1.9 collective-permute-start.1
  335.4 2.2 fusion.139
  337.6 10.0 %collective-permute-done.1 = bf16[192,1024]{0,1:T(8,128)(2,1)} collective-permute-done((bf16[192,1024]{0,1:T(8,128)(2,1)}, bf16[192,1024]{0,1:T(8,128)(2,1)}, u32[]{:S(2)}, u32[]{:S(2)}) %collective-permute-start.1) | collective-permute-done | bytes 393248 | tf_op jit(solution)/shard_map/while/body/eval_jaxpr/ppermute | solution.py:17
  354.1 5.3 collective-permute-start.1
  359.4 2.2 fusion.139
  361.6 6.5 %collective-permute-done.1 = bf16[192,1024]{0,1:T(8,128)(2,1)} collective-permute-done((bf16[192,1024]{0,1:T(8,128)(2,1)}, bf16[192,1024]{0,1:T(8,128)(2,1)}, u32[]{:S(2)}, u32[]{:S(2)}) %collective-permute-start.1) | collective-permute-done | bytes 393248 | tf_op jit(solution)/shard_map/while/body/eval_jaxpr/ppermute | solution.py:17
  374.5 8.4 %collective-permute-start.1 = (bf16[192,1024]{0,1:T(8,128)(2,1)}, bf16[192,1024]{0,1:T(8,128)(2,1)}, u32[]{:S(2)}, u32[]{:S(2)}) collective-permute-start(bf16[192,1024]{0,1:T(8,128)(2,1)} %fusion.138), channel_id=1, source_target_pairs={{1,0},{2,1},{3,2},{4,3},{5,4},{6,5},{7,6},{8,7},{9,8},{10,9},{11,1... | collective-permute-start | bytes 1179656 | tf_op jit(solution)/shard_map/while/body/eval_jaxpr/ppermute | solution.py:17
  382.9 2.2 fusion.139
  385.1 5.4 collective-permute-done.1
  395.8 215.8 %all-reduce.3.cloned.1.call-done = (f32[512,1024]{1,0:T(8,128)}, f32[31,1024]{1,0:T(8,128)}) async-done(((f32[512,1024]{1,0:T(8,128)}, f32[31,1024]{1,0:T(8,128)}), (f32[512,1024]{1,0:T(8,128)}, f32[31,1024]{1,0:T(8,128)})) %all-reduce.3.cloned.1.call-update) | async-done | bytes 2224144 | tf_op jit(solution)/shard_map/psum | solution.py:111
  611.6 3.2 copy.121
  (331 shorter events, 166.6 us)
Async XLA Ops:
  7.2 75.2 %copy-start = (bf16[512,1024]{1,0:T(8,128)(2,1)S(1)}, bf16[512,1024]{1,0:T(8,128)(2,1)}, u32[]{:S(2)}) copy-start(bf16[512,1024]{1,0:T(8,128)(2,1)} %param.19) | copy-start | bytes 3145732
  7.2 604.5 %all-reduce.3.cloned.1.call-start = ((), (), s32[]{:S(2)}) async-start(), calls=%async_computation | async-start | bytes 4456448 | tf_op jit(solution)/shard_map/psum | solution.py:111
  8.6 3.1 copy-start.10
  11.3 1.1 copy-start.1
  12.4 25.2 %collective-permute-start = (bf16[192,1024]{0,1:T(8,128)(2,1)S(1)}, bf16[192,1024]{0,1:T(8,128)(2,1)S(1)}, u32[]{:S(2)}, u32[]{:S(2)}) collective-permute-start(bf16[192,1024]{0,1:T(8,128)(2,1)S(1)} %get-tuple-element.1015), channel_id=1, source_target_pairs={{0,1},{1,2},{2,3},{3,4},{4,5},{5,6},{6,7},{7,8},{8,9},{9,10},{10,1... | collective-permute-start | bytes 1179656 | tf_op jit(solution)/shard_map/while/body/eval_jaxpr/ppermute | solution.py:17
  39.8 19.5 %collective-permute-start = (bf16[192,1024]{0,1:T(8,128)(2,1)S(1)}, bf16[192,1024]{0,1:T(8,128)(2,1)S(1)}, u32[]{:S(2)}, u32[]{:S(2)}) collective-permute-start(bf16[192,1024]{0,1:T(8,128)(2,1)S(1)} %get-tuple-element.1015), channel_id=1, source_target_pairs={{0,1},{1,2},{2,3},{3,4},{4,5},{5,6},{6,7},{7,8},{8,9},{9,10},{10,1... | collective-permute-start | bytes 1179656 | tf_op jit(solution)/shard_map/while/body/eval_jaxpr/ppermute | solution.py:17
  61.5 18.6 %collective-permute-start = (bf16[192,1024]{0,1:T(8,128)(2,1)S(1)}, bf16[192,1024]{0,1:T(8,128)(2,1)S(1)}, u32[]{:S(2)}, u32[]{:S(2)}) collective-permute-start(bf16[192,1024]{0,1:T(8,128)(2,1)S(1)} %get-tuple-element.1015), channel_id=1, source_target_pairs={{0,1},{1,2},{2,3},{3,4},{4,5},{5,6},{6,7},{7,8},{8,9},{9,10},{10,1... | collective-permute-start | bytes 1179656 | tf_op jit(solution)/shard_map/while/body/eval_jaxpr/ppermute | solution.py:17
  82.3 2.5 copy-start.7
  82.4 2.5 copy-start.12
  82.8 2.0 copy-start.15
  82.8 10.7 %collective-permute-start.2 = (bf16[30,1024]{1,0:T(8,128)(2,1)S(1)}, bf16[30,1024]{1,0:T(8,128)(2,1)S(1)}, u32[]{:S(2)}, u32[]{:S(2)}) collective-permute-start(bf16[30,1024]{1,0:T(8,128)(2,1)S(1)} %slice.52), channel_id=1, source_target_pairs={{0,1},{1,2},{2,3},{3,4},{4,5},{5,6},{6,7},{7,8},{8,9},{9,10},{10,1... | collective-permute-start | bytes 184328 | tf_op jit(solution)/shard_map/ppermute | solution.py:17
  130.9 0.9 copy-start.8
  134.1 108.3 %collective-permute-start.3 = (bf16[30,1024]{1,0:T(8,128)(2,1)S(1)}, bf16[30,1024]{1,0:T(8,128)(2,1)S(1)}, u32[]{:S(2)}, u32[]{:S(2)}) collective-permute-start(bf16[30,1024]{1,0:T(8,128)(2,1)S(1)} %slice.59), channel_id=1, source_target_pairs={{1,0},{2,1},{3,2},{4,3},{5,4},{6,5},{7,6},{8,7},{9,8},{10,9},{11,1... | collective-permute-start | bytes 184328 | tf_op jit(solution)/shard_map/ppermute | solution.py:17
  242.4 1.5 copy-start.3
  315.0 0.9 copy-start.4
  315.9 4.6 copy-start.2
  321.8 0.9 copy-start.11
  322.7 1.4 copy-start.5
  322.7 1.4 copy-start.13
  324.2 1.8 copy-start.14
  326.9 1.4 copy-start.6
  330.6 0.8 copy-start.9
  333.5 14.1 %collective-permute-start.1 = (bf16[192,1024]{0,1:T(8,128)(2,1)}, bf16[192,1024]{0,1:T(8,128)(2,1)}, u32[]{:S(2)}, u32[]{:S(2)}) collective-permute-start(bf16[192,1024]{0,1:T(8,128)(2,1)} %fusion.138), channel_id=1, source_target_pairs={{1,0},{2,1},{3,2},{4,3},{5,4},{6,5},{7,6},{8,7},{9,8},{10,9},{11,1... | collective-permute-start | bytes 1179656 | tf_op jit(solution)/shard_map/while/body/eval_jaxpr/ppermute | solution.py:17
  351.2 0.8 copy-start.9
  354.1 14.0 %collective-permute-start.1 = (bf16[192,1024]{0,1:T(8,128)(2,1)}, bf16[192,1024]{0,1:T(8,128)(2,1)}, u32[]{:S(2)}, u32[]{:S(2)}) collective-permute-start(bf16[192,1024]{0,1:T(8,128)(2,1)} %fusion.138), channel_id=1, source_target_pairs={{1,0},{2,1},{3,2},{4,3},{5,4},{6,5},{7,6},{8,7},{9,8},{10,9},{11,1... | collective-permute-start | bytes 1179656 | tf_op jit(solution)/shard_map/while/body/eval_jaxpr/ppermute | solution.py:17
  371.6 0.8 copy-start.9
  374.5 16.0 %collective-permute-start.1 = (bf16[192,1024]{0,1:T(8,128)(2,1)}, bf16[192,1024]{0,1:T(8,128)(2,1)}, u32[]{:S(2)}, u32[]{:S(2)}) collective-permute-start(bf16[192,1024]{0,1:T(8,128)(2,1)} %fusion.138), channel_id=1, source_target_pairs={{1,0},{2,1},{3,2},{4,3},{5,4},{6,5},{7,6},{8,7},{9,8},{10,9},{11,1... | collective-permute-start | bytes 1179656 | tf_op jit(solution)/shard_map/while/body/eval_jaxpr/ppermute | solution.py:17
  611.6 3.2 copy-start.16
Sparse Core Ops, SparseCore 0:
  328.0 283.6 all-reduce.2
where the time goes:
time: 632 us; the launch traced here: 622 us
  waiting for transfers between devices  297 us (47%)
  local copies, waits for them, and re-layouts  134 us (21%)
  other arithmetic  79.2 us (13%)
  loops' own time  46.3 us (7%)
  starting transfers between devices  28.2 us (4%)
  matrix products  23.3 us (4%)
  between operations  14.4 us (2%)
    psum x1, waiting for transfers between devices, sum_weights(): return lax.psum((weight_part, kernel_part), ('dp', 'blk'))  216 us
    ppermute x8, waiting for transfers between devices, from_behind(): return lax.ppermute(block, axis, route)  81.1 us
    add x62, other arithmetic, add_tap(): running + conv_kernel[tap_index] * lax.dynamic_slice_in_dim(extended, fir...  58.3 us
    dynamic_slice x62, local copies, waits for them, and re-layouts, add_tap(): conv_kernel[tap_index]  47.7 us
    dynamic_update_slice x31, local copies, waits for them, and re-layouts, per_device(): lax.map(kernel_tap, jnp.arange(edge_rows + 1, dtype=jnp.int32))  43.4 us
    another operation x1, loops' own time, per_device(): lax.map(kernel_tap, jnp.arange(edge_rows + 1, dtype=jnp.int32))  40.4 us
    ppermute x8, starting transfers between devices, from_behind(): return lax.ppermute(block, axis, route)  28.1 us
    dynamic_slice x31, local copies, waits for them, and re-layouts, per_device(): lax.map(kernel_tap, jnp.arange(edge_rows + 1, dtype=jnp.int32))  18 us
  transfers between devices with their start and end apart: 9, of which 8 were waited for; matrix products, arithmetic and copies ran while one was open for 15% of the time, Pallas kernels for 0%

commit v1 on v0

--- a/solution.py
+++ b/solution.py
@@ -108,7 +108,7 @@
 
 
 def sum_weights(weight_part, kernel_part):
-    return lax.psum((weight_part, kernel_part), ("dp", "blk"))
+    return lax.psum(lax.psum((weight_part, kernel_part), axis_name="dp"), axis_name="blk")
 
 
 def per_device(queries, key_in, value_in, out_weight, conv_kernel, cotangent):

time: 632 us -> 1760 us (2.78)
  the two profiles are of different devices: /device:TPU:24 before, /device:TPU:32 now
where the time goes in v1:
time: 1760 us; the launch traced here: 1750 us
  waiting for transfers between devices  1410 us (80%)
  local copies, waits for them, and re-layouts  134 us (8%)
  other arithmetic  79.1 us (4%)
  loops' own time  46.3 us (3%)
  starting transfers between devices  41 us (2%)
  matrix products  24.5 us (1%)
    psum x1, waiting for transfers between devices, sum_weights(): lax.psum(lax.psum((weight_part, kernel_part), axis_name='dp'), axis_name=...  1260 us
    ppermute x8, waiting for transfers between devices, from_behind(): return lax.ppermute(block, axis, route)  89.7 us
    add x62, other arithmetic, add_tap(): running + conv_kernel[tap_index] * lax.dynamic_slice_in_dim(extended, fir...  58.3 us
    psum x1, waiting for transfers between devices, sum_weights(): lax.psum((weight_part, kernel_part), axis_name='dp')  53.9 us
    dynamic_slice x62, local copies, waits for them, and re-layouts, add_tap(): conv_kernel[tap_index]  47.7 us
    dynamic_update_slice x31, local copies, waits for them, and re-layouts, per_device(): lax.map(kernel_tap, jnp.arange(edge_rows + 1, dtype=jnp.int32))  43.4 us
    ppermute x8, starting transfers between devices, from_behind(): return lax.ppermute(block, axis, route)  40.9 us
    another operation x1, loops' own time, per_device(): lax.map(kernel_tap, jnp.arange(edge_rows + 1, dtype=jnp.int32))  40.4 us
  transfers between devices with their start and end apart: 10, of which 9 were waited for; matrix products, arithmetic and copies ran while one was open for 6% of the time, Pallas kernels for 0%

profile of v1, /device:TPU:32, one launch (start us, length us, event | category | flops | bytes accessed | tf_op | source)
XLA Modules:
  0.0 1746.4 jit_solution(14839362597210874129)
XLA Ops:
  12.4 72.3 %while.79 = (s32[]{:T(128)}, bf16[192,1024]{0,1:T(8,128)(2,1)S(1)}, f32[8,192]{1,0:T(8,128)S(1)}, f32[8,192]{1,0:T(8,128)S(1)}, f32[192,8,64]{0,2,1:T(8,128)S(1)...) while((s32[]{:T(128)}, bf16[192,1024]{0,1:T(8,128)(2,1)S(1)}, ...), condition=%wide.region_5.6_spmd.clone, body=%wide.region_2.5_spmd.clone.sunk | while | flops 78537600 | bytes 9227495 | solution.py:158
  12.4 4.9 collective-permute-start
  18.7 18.9 %collective-permute-done = bf16[192,1024]{0,1:T(8,128)(2,1)S(1)} collective-permute-done((bf16[192,1024]{0,1:T(8,128)(2,1)S(1)}, bf16[192,1024]{0,1:T(8,128)(2,1)S(1)}, u32[]{:S(2)}, u32[]{:S(2)}) %collective-permute-start) | collective-permute-done | bytes 393248 | tf_op jit(solution)/shard_map/while/body/eval_jaxpr/ppermute | solution.py:17
  39.8 1.9 collective-permute-start
  43.1 17.4 collective-permute-done
  62.7 1.9 collective-permute-start
  66.0 16.5 collective-permute-done
  85.2 1.9 collective-permute-start.2
  87.2 9.9 collective-permute-done.2
  98.2 36.2 %while.80 = (s32[]{:T(128)}, f32[192,1024]{1,0:T(8,128)S(1)}, f32[31,1024]{1,0:T(8,128)}, f32[222,1024]{1,0:T(8,128)S(1)}, s32[]{:T(128)}, /*index=5*/s32[]{:T(128)}, s32[]{:T(128)}, s32[]{:T(128)}) while((s32[]{:T(128)}, f32[192,1024]{1,0:T(8,128)S(1)}, f32[31,1024]{1,0:T(8,128)}, f32[222,1024]{1,0:T(8,128)S(1)}, s32[]{:T(128)}, ...), condition=%wide.region_7.8_spmd.clone, body=%wide.region_6.7_spmd.clone.sunk | while | flops 589831 | bytes 2371741 | solution.py:107
  135.4 2.3 fusion.39
  137.7 1.9 collective-permute-start.3
  139.6 106.3 %while.78 = (s32[]{:T(128)}, f32[31,1024]{1,0:T(8,128)}, s32[31]{0:T(128)S(1)}, f32[222,1024]{1,0:T(8,128)S(1)}, f32[192,1024]{1,0:T(8,128)S(1)}, /*index=5*/s32[]{:T(128)}, s32[1]{0:T(128)}, s32[]{:T(128)}, s32[1]{0:T(128)}) while((s32[]{:T(128)}, f32[31,1024]{1,0:T(8,128)}, s32[31]{0:T(128)S(1)}, f32[222,1024]{1,0:T(8,128)S(1)}, ...), condition=%wide.region_16.17_spmd, body=%wide.region_14.16_spmd.sunk | while | flops 392198 | bytes 1585319 | solution.py:181
  141.7 1.4 dynamic_update_slice.15
  148.5 1.4 dynamic_update_slice.15
  247.4 71.2 %while.81 = (s32[]{:T(128)}, f32[192,1024]{1,0:T(8,128)S(1)}, f32[31,1024]{1,0:T(8,128)}, f32[222,1024]{1,0:T(8,128)}, s32[]{:T(128)}, /*index=5*/s32[]{:T(128)}) while((s32[]{:T(128)}, f32[192,1024]{1,0:T(8,128)S(1)}, f32[31,1024]{1,0:T(8,128)}, f32[222,1024]{1,0:T(8,128)}, s32[]{:T(128)}, /*index=5*/s32[]{:T(128)}) %tuple.193), condition=%wide.region_9.10_spmd.clone, body=%wide.region_8.9_spmd.clone.sunk | while | flops 589827 | bytes 2371679 | solution.py:107
  248.2 1.5 select_add_fusion.5
  250.5 1.5 select_add_fusion.5
  252.8 1.5 select_add_fusion.5
  255.1 1.5 select_add_fusion.5
  257.4 1.5 select_add_fusion.5
  259.7 1.5 select_add_fusion.5
  262.0 1.5 select_add_fusion.5
  264.3 1.5 select_add_fusion.5
  266.6 1.5 select_add_fusion.5
  268.9 1.5 select_add_fusion.5
  271.2 1.5 select_add_fusion.5
  273.5 1.5 select_add_fusion.5
  275.8 1.5 select_add_fusion.5
  278.1 1.5 select_add_fusion.5
  280.4 1.5 select_add_fusion.5
  282.6 1.5 select_add_fusion.5
  284.9 1.5 select_add_fusion.5
  287.2 1.5 select_add_fusion.5
  289.5 1.5 select_add_fusion.5
  291.8 1.5 select_add_fusion.5
  294.1 1.5 select_add_fusion.5
  296.4 1.5 select_add_fusion.5
  298.7 1.5 select_add_fusion.5
  301.0 1.5 select_add_fusion.5
  303.3 1.5 select_add_fusion.5
  305.6 1.5 select_add_fusion.5
  307.9 1.5 select_add_fusion.5
  310.2 1.5 select_add_fusion.5
  312.5 1.5 select_add_fusion.5
  314.8 1.5 select_add_fusion.5
  317.1 1.5 select_add_fusion.5
  318.6 1.8 fusion.48
  320.5 2.4 convolution_convert_fusion.1
  325.2 2.0 copy.51
  331.1 2.3 fusion.33
  333.4 53.9 %all-reduce.7.cloned.1.call-done = (f32[512,1024]{1,0:T(8,128)}, f32[31,1024]{1,0:T(8,128)}) async-done(((f32[512,1024]{1,0:T(8,128)}, f32[31,1024]{1,0:T(8,128)}), (f32[512,1024]{1,0:T(8,128)}, f32[31,1024]{1,0:T(8,128)})) %all-reduce.7.cloned.1.call-update) | async-done | bytes 2224144 | tf_op jit(solution)/shard_map/psum | solution.py:111
  387.4 81.2 %while.82 = (s32[]{:T(128)}, f32[192,1024]{0,1:T(8,128)S(1)}, f32[192,8,64]{0,2,1:T(8,128)}, s32[3]{0:T(128)S(1)}, s32[]{:T(128)}, /*index=5*/bf16[3,192,1024]{1...) while((s32[]{:T(128)}, f32[192,1024]{0,1:T(8,128)S(1)}, ...), condition=%wide.region_11.12_spmd.clone, body=%wide.region_10.11_spmd.clone.sunk | while | flops 192565632 | bytes 15424801 | solution.py:223
  392.6 8.0 collective-permute-start.1
  400.6 2.2 fusion.139
  402.8 10.0 collective-permute-done.1
  419.2 10.2 collective-permute-start.1
  429.4 2.2 fusion.139
  431.6 8.9 collective-permute-done.1
  446.9 10.2 collective-permute-start.1
  457.1 2.2 fusion.139
  459.3 8.1 collective-permute-done.1
  472.7 1263.0 %all-reduce.5.cloned.1.call-done = (f32[512,1024]{1,0:T(8,128)}, f32[31,1024]{1,0:T(8,128)}) async-done(((f32[512,1024]{1,0:T(8,128)}, f32[31,1024]{1,0:T(8,128)}), (f32[512,1024]{1,0:T(8,128)}, f32[31,1024]{1,0:T(8,128)})) %all-reduce.5.cloned.1.call-update) | async-done | bytes 2224144 | tf_op jit(solution)/shard_map/psum | solution.py:111
  1735.7 3.2 copy.123
  (332 shorter events, 168.1 us)
Async XLA Ops:
  7.2 77.6 %copy-start = (bf16[512,1024]{1,0:T(8,128)(2,1)S(1)}, bf16[512,1024]{1,0:T(8,128)(2,1)}, u32[]{:S(2)}) copy-start(bf16[512,1024]{1,0:T(8,128)(2,1)} %param.19) | copy-start | bytes 3145732
  7.2 380.1 %all-reduce.7.cloned.1.call-start = ((), (), s32[]{:S(2)}) async-start(), calls=%async_computation.1 | async-start | bytes 4456448 | tf_op jit(solution)/shard_map/psum | solution.py:111
  8.6 3.1 copy-start.10
  11.3 1.1 copy-start.1
  12.4 25.2 %collective-permute-start = (bf16[192,1024]{0,1:T(8,128)(2,1)S(1)}, bf16[192,1024]{0,1:T(8,128)(2,1)S(1)}, u32[]{:S(2)}, u32[]{:S(2)}) collective-permute-start(bf16[192,1024]{0,1:T(8,128)(2,1)S(1)} %get-tuple-element.1017), channel_id=1, source_target_pairs={{0,1},{1,2},{2,3},{3,4},{4,5},{5,6},{6,7},{7,8},{8,9},{9,10},{10,1... | collective-permute-start | bytes 1179656 | tf_op jit(solution)/shard_map/while/body/eval_jaxpr/ppermute | solution.py:17
  39.8 20.7 %collective-permute-start = (bf16[192,1024]{0,1:T(8,128)(2,1)S(1)}, bf16[192,1024]{0,1:T(8,128)(2,1)S(1)}, u32[]{:S(2)}, u32[]{:S(2)}) collective-permute-start(bf16[192,1024]{0,1:T(8,128)(2,1)S(1)} %get-tuple-element.1017), channel_id=1, source_target_pairs={{0,1},{1,2},{2,3},{3,4},{4,5},{5,6},{6,7},{7,8},{8,9},{9,10},{10,1... | collective-permute-start | bytes 1179656 | tf_op jit(solution)/shard_map/while/body/eval_jaxpr/ppermute | solution.py:17
  62.7 19.8 %collective-permute-start = (bf16[192,1024]{0,1:T(8,128)(2,1)S(1)}, bf16[192,1024]{0,1:T(8,128)(2,1)S(1)}, u32[]{:S(2)}, u32[]{:S(2)}) collective-permute-start(bf16[192,1024]{0,1:T(8,128)(2,1)S(1)} %get-tuple-element.1017), channel_id=1, source_target_pairs={{0,1},{1,2},{2,3},{3,4},{4,5},{5,6},{6,7},{7,8},{8,9},{9,10},{10,1... | collective-permute-start | bytes 1179656 | tf_op jit(solution)/shard_map/while/body/eval_jaxpr/ppermute | solution.py:17
  84.7 2.5 copy-start.6
  84.8 2.4 copy-start.12
  85.2 2.0 copy-start.14
  85.2 11.9 collective-permute-start.2
  134.5 0.9 copy-start.7
  137.7 108.2 %collective-permute-start.3 = (bf16[30,1024]{1,0:T(8,128)(2,1)S(1)}, bf16[30,1024]{1,0:T(8,128)(2,1)S(1)}, u32[]{:S(2)}, u32[]{:S(2)}) collective-permute-start(bf16[30,1024]{1,0:T(8,128)(2,1)S(1)} %slice.59), channel_id=1, source_target_pairs={{1,0},{2,1},{3,2},{4,3},{5,4},{6,5},{7,6},{8,7},{9,8},{10,9},{11,1... | collective-permute-start | bytes 184328 | tf_op jit(solution)/shard_map/ppermute | solution.py:17
  245.9 1.5 copy-start.3
  247.4 71.2 %copy-start.13 = (bf16[192,8,64]{0,2,1:T(8,128)(2,1)S(1)}, bf16[192,8,64]{0,2,1:T(8,128)(2,1)}, u32[]{:S(2)}) copy-start(bf16[192,8,64]{0,2,1:T(8,128)(2,1)} %copy-done.12) | copy-start | bytes 589828
  318.6 1.8 copy-start.4
  320.4 3.6 copy-start.2
  320.4 1415.3 %all-reduce.5.cloned.1.call-start = ((), (), s32[]{:S(2)}) async-start(), calls=%async_computation | async-start | bytes 4456448 | tf_op jit(solution)/shard_map/psum | solution.py:111
  328.9 0.9 copy-start.9
  329.8 1.4 copy-start.11
  331.1 56.2 %copy-start.5 = (f32[192,1024]{0,1:T(8,128)S(1)}, f32[192,1024]{0,1:T(8,128)}, u32[]{:S(2)}) copy-start(f32[192,1024]{0,1:T(8,128)} %custom-call.2) | copy-start | bytes 2359300
  389.7 0.8 copy-start.8
  392.6 20.1 %collective-permute-start.1 = (bf16[192,1024]{0,1:T(8,128)(2,1)}, bf16[192,1024]{0,1:T(8,128)(2,1)}, u32[]{:S(2)}, u32[]{:S(2)}) collective-permute-start(bf16[192,1024]{0,1:T(8,128)(2,1)} %fusion.138), channel_id=1, source_target_pairs={{1,0},{2,1},{3,2},{4,3},{5,4},{6,5},{7,6},{8,7},{9,8},{10,9},{11,1... | collective-permute-start | bytes 1179656 | tf_op jit(solution)/shard_map/while/body/eval_jaxpr/ppermute | solution.py:17
  416.3 0.8 copy-start.8
  419.2 21.3 %collective-permute-start.1 = (bf16[192,1024]{0,1:T(8,128)(2,1)}, bf16[192,1024]{0,1:T(8,128)(2,1)}, u32[]{:S(2)}, u32[]{:S(2)}) collective-permute-start(bf16[192,1024]{0,1:T(8,128)(2,1)} %fusion.138), channel_id=1, source_target_pairs={{1,0},{2,1},{3,2},{4,3},{5,4},{6,5},{7,6},{8,7},{9,8},{10,9},{11,1... | collective-permute-start | bytes 1179656 | tf_op jit(solution)/shard_map/while/body/eval_jaxpr/ppermute | solution.py:17
  444.0 0.8 copy-start.8
  446.9 20.5 %collective-permute-start.1 = (bf16[192,1024]{0,1:T(8,128)(2,1)}, bf16[192,1024]{0,1:T(8,128)(2,1)}, u32[]{:S(2)}, u32[]{:S(2)}) collective-permute-start(bf16[192,1024]{0,1:T(8,128)(2,1)} %fusion.138), channel_id=1, source_target_pairs={{1,0},{2,1},{3,2},{4,3},{5,4},{6,5},{7,6},{8,7},{9,8},{10,9},{11,1... | collective-permute-start | bytes 1179656 | tf_op jit(solution)/shard_map/while/body/eval_jaxpr/ppermute | solution.py:17
  1735.7 3.2 copy-start.15
Sparse Core Ops, SparseCore 0:
  320.5 66.7 all-reduce.6
  390.3 1345.3 all-reduce.4
